TPU v7x, 256 devices: a whole 4x4x8 slice. The times are simulated.
256 devices in a mesh: dp: 2 (over y_hi), pipe: 16 (over y_lo, x, core), seq: 8 (over z).
Axes of the slice: x: 4, y: 4 (y_hi: 2, y_lo: 2; y = y_hi * 2 + y_lo), z: 8, core: 2. Of those that a mesh axis runs over, the one named last changes fastest.
Arguments:
- enc_out: bfloat16 [2, 512, 4096], P('dp', None, 'seq'), may hold values from -60 to 60
- w_key: bfloat16 [16, 4096, 2048], P('pipe', None, 'seq'), may hold values from -0.125 to 0.125
- w_value: bfloat16 [16, 4096, 2048], P('pipe', None, 'seq'), may hold values from -0.125 to 0.125
- query: bfloat16 [16, 2, 512, 2048], P('pipe', 'dp', None, 'seq'), may hold values from -256 to 256
- key_cache: bfloat16 [16, 2, 512, 2048], P('pipe', 'dp', None, 'seq'), may hold values from -6 to 6
- value_cache: bfloat16 [16, 2, 512, 2048], P('pipe', 'dp', None, 'seq'), may hold values from -6 to 6
- grad_attn: bfloat16 [16, 2, 512, 2048], P('pipe', 'dp', None, 'seq'), may hold values from -200 to 200
- dec_segments: int32 [2, 512], P('dp'), may hold values from 0 to 3, as said below
- enc_segments: int32 [2, 512], P('dp'), may hold values from 0 to 3, as said below
Outputs:
- grad_query: bfloat16 [16, 2, 512, 2048], P('pipe', 'dp', None, 'seq')
- grad_enc: float32 [2, 512, 4096], P('dp', 'seq', 'pipe')
- grad_wkey: float32 [16, 4096, 2048], P('pipe', 'dp', 'seq')
- grad_wvalue: float32 [16, 4096, 2048], P('pipe', 'dp', 'seq')
Inputs may be any that keep to these rules, and one draw needn't show every extreme that they name: `dec_segments`: never falling along a sequence; every number from 0 to 3 occurs; a segment holds 1 to 256 tokens, and one holds exactly 256. `enc_segments`: never falling along a sequence; every number from 0 to 3 occurs; a segment holds 1 to 256 tokens, and one holds exactly 256.
All inputs are finite; a program needn't handle non-finite values.
Results may differ from a plain program's by a relative error of at most 0.006.
Values may be sent and summed in bfloat16 or wider, within the bound.
No kernel may reach another device: no remote copies, remote signals or barrier semaphores. Data moves between devices by JAX's collectives and lax.ppermute only.
A program may use at most 128 MiB of HBM per device.

v0:
```python
import math
import jax
import jax.numpy as jnp
from jax import lax
from jax.sharding import PartitionSpec as P

D = 4096
H = 8
HD = 256


def head_backward(query_heads, key_heads, value_heads, grad_heads, dec_ids, enc_ids):
    length = query_heads.shape[0]
    block_rows = 512
    block_count = length // block_rows
    inverse_root = 1.0 / math.sqrt(query_heads.shape[2])

    def block_step(partial_value, block_index):
        acc_key, acc_value = partial_value
        same_segment = dec_ids[:, None] == enc_ids[None, :]
        scores = (
            jnp.einsum("qhd,khd->hqk", query_heads, key_heads, preferred_element_type=jnp.float32)
            * inverse_root
        )
        scores = jnp.where(same_segment[None], scores, -jnp.inf)
        row_max = jnp.max(scores, axis=2, keepdims=True)
        exp_scores = jnp.exp(scores - row_max)
        probs_full = exp_scores / jnp.sum(exp_scores, axis=2, keepdims=True)
        dprobs = jnp.einsum(
            "qhd,khd->hqk", grad_heads, value_heads, preferred_element_type=jnp.float32
        )
        row_delta = jnp.sum(probs_full * dprobs, axis=2, keepdims=True)
        dscores = (probs_full * (dprobs - row_delta) * inverse_root).astype(jnp.bfloat16)
        probs_low = probs_full.astype(jnp.bfloat16)
        query_grad = jnp.einsum(
            "hqk,khd->qhd", dscores, key_heads, preferred_element_type=jnp.float32
        ).astype(jnp.bfloat16)
        acc_key = acc_key + jnp.einsum(
            "hqk,qhd->khd", dscores, query_heads, preferred_element_type=jnp.float32
        )
        acc_value = acc_value + jnp.einsum(
            "hqk,qhd->khd", probs_low, grad_heads, preferred_element_type=jnp.float32
        )
        return ((acc_key, acc_value), query_grad)

    zeros_init = jnp.zeros(key_heads.shape, jnp.float32)
    (acc_key, acc_value), query_blocks = lax.scan(
        block_step, (zeros_init, zeros_init), jnp.arange(block_count, dtype=jnp.int32)
    )
    query_grad = query_blocks.reshape(query_heads.shape)
    return (query_grad, acc_key.astype(jnp.bfloat16), acc_value.astype(jnp.bfloat16))


def shards(
    enc_out, w_key, w_value, query, key_cache, value_cache, grad_attn, dec_segments, enc_segments
):
    length = query.shape[2]
    columns = query.shape[3]
    local_heads = columns // HD
    head_shape = (length, local_heads, HD)
    query_grad, grad_keys, grad_values = head_backward(
        query[0, 0].reshape(head_shape),
        key_cache[0, 0].reshape(head_shape),
        value_cache[0, 0].reshape(head_shape),
        grad_attn[0, 0].reshape(head_shape),
        dec_segments[0],
        enc_segments[0],
    )
    grad_query = query_grad.reshape(1, 1, length, columns)
    keys_flat = grad_keys.reshape(length, columns)
    values_flat = grad_values.reshape(length, columns)
    section_wkey = w_key[0]
    section_wvalue = w_value[0]
    column_contract = (((1,), (1,)), ((), ()))
    by_section = lax.psum_scatter(
        lax.dot_general(
            section_wkey, keys_flat, column_contract, preferred_element_type=jnp.float32
        )
        + lax.dot_general(
            section_wvalue, values_flat, column_contract, preferred_element_type=jnp.float32
        ),
        "pipe",
        scatter_dimension=0,
        tiled=True,
    )
    by_head = lax.psum_scatter(by_section, "seq", scatter_dimension=1, tiled=True)
    grad_enc = jnp.transpose(by_head)[None]
    token_contract = (((0,), (0,)), ((), ()))
    grad_both = jnp.concatenate([keys_flat, values_flat], axis=1)
    both_sums = lax.dot_general(
        lax.all_gather(enc_out, "seq", axis=2, tiled=True)[0],
        grad_both,
        token_contract,
        preferred_element_type=jnp.float32,
    )
    sum_key = both_sums[:, :columns]
    sum_value = both_sums[:, columns:]
    share_key, share_value = (
        lax.psum_scatter(sum_key, "dp", scatter_dimension=0, tiled=True),
        lax.psum_scatter(sum_value, "dp", scatter_dimension=0, tiled=True),
    )
    square_key, square_value = lax.psum(
        (jnp.sum(share_key * share_key), jnp.sum(share_value * share_value)), ("dp", "seq")
    )
    entries = D * H * HD
    grad_wkey = (share_key / jnp.sqrt(square_key / entries + 1e-06))[None]
    grad_wvalue = (share_value / jnp.sqrt(square_value / entries + 1e-06))[None]
    return (grad_query, grad_enc, grad_wkey, grad_wvalue)


def solution(mesh):
    in_specs = (
        P("dp", None, "seq"),
        P("pipe", None, "seq"),
        P("pipe", None, "seq"),
        P("pipe", "dp", None, "seq"),
        P("pipe", "dp", None, "seq"),
        P("pipe", "dp", None, "seq"),
        P("pipe", "dp", None, "seq"),
        P("dp", None),
        P("dp", None),
    )
    out_specs = (
        P("pipe", "dp", None, "seq"),
        P("dp", "seq", "pipe"),
        P("pipe", "dp", "seq"),
        P("pipe", "dp", "seq"),
    )
    return jax.shard_map(shards, mesh=mesh, in_specs=in_specs, out_specs=out_specs, check_vma=False)
```

profile of v0, /device:TPU:4, one launch (start us, length us, event | category | flops | bytes accessed | tf_op | source)
XLA Modules:
  0.0 323.7 jit_solution(271857215477745825)
XLA Ops:
  7.2 0.0 copy-start
  7.2 0.0 copy-start.3
  7.2 0.0 copy-start.4
  7.2 0.0 all-gather.2.cloned.1.call-start
  7.2 0.7 all-gather.2.cloned.1.call-update
  7.9 0.0 reduce-scatter.9.cloned.1.call-start
  8.0 1.4 fusion.23
  9.4 0.2 fusion.7
  9.6 0.0 copy-done.3
  9.6 0.0 copy-done.4
  9.6 0.4 multiply_reduce_fusion.2
  9.9 0.0 copy-start.2
  10.0 0.3 multiply_convert_fusion
  10.2 0.6 copy-done.2
  10.9 0.3 convolution_convert_fusion.1
  11.2 0.4 convolution_convert_fusion
  11.7 55.8 %all-gather.2.cloned.1.call-done = bf16[1,512,4096]{2,1,0:T(8,128)(2,1)} async-done(((bf16[1,512,512]{2,1,0:T(8,128)(2,1)}), bf16[1,512,4096]{2,1,0:T(8,128)(2,1)}) %all-gather.2.cloned.1.call-update) | async-done | bytes 4194320 | tf_op jit(solution)/shard_map/all_gather | solution.py:91
  67.5 4.5 %convolution_bitcast_fusion = f32[4096,512]{0,1:T(8,128)S(1)} fusion(bf16[1,512,4096]{2,1,0:T(8,128)(2,1)} %all-gather.2.cloned.1.call-done, bf16[512,256]{0,1:T(8,128)(2,1)S(1)} %convolution_convert_fusion, bf16[512,256]{0,1:T(8,128)(2,1)S(1)} %convolution_convert_fusion.1), kind=kOutput, calls=%fused_computation.1 | convolution fusion | flops 2148532224 | bytes 13107200 | tf_op jit(solution)/shard_map/dot_general | solution.py:90
  72.1 3.8 %fusion.22 = (f32[4096,256]{0,1:T(8,128)}, f32[4096,256]{0,1:T(8,128)}) fusion(f32[4096,512]{0,1:T(8,128)S(1)} %convolution_bitcast_fusion), kind=kLoop, calls=%fused_computation.34 | loop fusion | bytes 16777216 | tf_op jit(solution)/shard_map/slice | solution.py:97
  75.8 0.0 reduce-scatter.9.cloned.1.call-update
  75.8 0.0 reduce-scatter.11.cloned.1.call-start
  75.9 0.7 reduce-scatter.11.cloned.1.call-update
  76.6 0.0 reduce-scatter.5.cloned.1.call-start
  76.6 0.0 copy-done
  76.6 0.0 copy-start.1
  76.6 1.3 fusion.2
  77.9 0.3 copy-done.1
  78.2 4.5 %add_bitcast_fusion = f32[4096,512]{0,1:T(8,128)} fusion(f32[512,4096]{1,0:T(8,128)S(1)} %fusion.2, bf16[512,256]{0,1:T(8,128)(2,1)S(1)} %convolution_convert_fusion, bf16[1,4096,256]{2,1,0:T(8,128)(2,1)S(1)} %copy-done.1), kind=kOutput, calls=%fused_computation | convolution fusion | flops 1075838976 | bytes 19136512 | tf_op jit(solution)/shard_map/dot_general | solution.py:79
  82.8 0.0 reduce-scatter.5.cloned.1.call-update
  82.8 0.0 copy-start.5
  82.8 0.0 reduce-scatter.7.cloned.1.call-start
  82.8 52.7 %reduce-scatter.9.cloned.1.call-done = f32[2048,256]{0,1:T(8,128)} async-done(((f32[4096,256]{0,1:T(8,128)}), f32[2048,256]{0,1:T(8,128)}) %reduce-scatter.9.cloned.1.call-update) | async-done | bytes 2097168 | tf_op jit(solution)/shard_map/reduce_scatter | solution.py:99
  135.6 2.7 multiply_reduce_fusion.1
  138.3 60.3 %reduce-scatter.11.cloned.1.call-done = f32[2048,256]{0,1:T(8,128)} async-done(((f32[4096,256]{0,1:T(8,128)}), f32[2048,256]{0,1:T(8,128)}) %reduce-scatter.11.cloned.1.call-update) | async-done | bytes 2097168 | tf_op jit(solution)/shard_map/reduce_scatter | solution.py:100
  198.6 2.7 multiply_reduce_fusion
  201.3 0.0 copy-done.5
  201.3 1.1 fusion.5
  202.4 40.5 %all-reduce = (f32[]{:T(128)}, f32[]{:T(128)}) all-reduce(f32[]{:T(128)} %multiply_reduce_fusion.1, f32[]{:T(128)} %multiply_reduce_fusion), channel_id=1, replica_groups=mesh['dp'=2,'pipe'=16,'seq'=8] {'dp','seq'}, use_global_device_ids=true, to_apply=%region_7.8 | all-reduce | flops 2 | bytes 16 | tf_op jit(solution)/shard_map/psum | solution.py:102
  243.6 26.8 %reduce-scatter.5.cloned.1.call-done = f32[256,512]{0,1:T(8,128)} async-done(((f32[4096,512]{0,1:T(8,128)}), f32[256,512]{0,1:T(8,128)}) %reduce-scatter.5.cloned.1.call-update) | async-done | bytes 524304 | tf_op jit(solution)/shard_map/reduce_scatter | solution.py:75
  270.4 0.0 reduce-scatter.7.cloned.1.call-update
  270.4 3.2 divide_bitcast_fusion.1
  273.6 2.9 copy.13
  277.1 3.2 divide_bitcast_fusion
  280.4 2.9 copy.14
  283.2 33.9 %reduce-scatter.7.cloned.1.call-done = f32[256,64]{0,1:T(8,128)} async-done(((f32[256,512]{0,1:T(8,128)}), f32[256,64]{0,1:T(8,128)}) %reduce-scatter.7.cloned.1.call-update) | async-done | bytes 65552 | tf_op jit(solution)/shard_map/reduce_scatter | solution.py:86
Async XLA Ops:
  7.2 69.5 %copy-start = (bf16[1,4096,256]{2,1,0:T(8,128)(2,1)S(1)}, bf16[1,4096,256]{2,1,0:T(8,128)(2,1)}, u32[]{:S(2)}) copy-start(bf16[1,4096,256]{2,1,0:T(8,128)(2,1)} %param.10) | copy-start | bytes 6291460
  7.2 2.4 copy-start.3
  7.2 2.4 copy-start.4
  7.2 60.3 %all-gather.2.cloned.1.call-start = ((), (), s32[]{:S(2)}) async-start(), calls=%async_computation.6 | async-start | bytes 4718592 | tf_op jit(solution)/shard_map/all_gather | solution.py:91
  7.9 127.6 %reduce-scatter.9.cloned.1.call-start = ((), (), s32[]{:S(2)}) async-start(), calls=%async_computation.7 | async-start | bytes 6291456 | tf_op jit(solution)/shard_map/reduce_scatter | solution.py:99
  9.9 1.0 copy-start.2
  75.8 122.7 %reduce-scatter.11.cloned.1.call-start = ((), (), s32[]{:S(2)}) async-start(), calls=%async_computation.8 | async-start | bytes 6291456 | tf_op jit(solution)/shard_map/reduce_scatter | solution.py:100
  76.6 193.8 %reduce-scatter.5.cloned.1.call-start = ((), (), s32[]{:S(2)}) async-start(), calls=%async_computation.4 | async-start | bytes 8912896 | tf_op jit(solution)/shard_map/reduce_scatter | solution.py:75
  76.6 1.6 copy-start.1
  82.8 118.5 %copy-start.5 = (bf16[1,1,512,256]{3,2,1,0:T(8,128)(2,1)S(1)}, bf16[1,1,512,256]{3,2,1,0:T(8,128)(2,1)}, u32[]{:S(2)}) copy-start(bf16[1,1,512,256]{3,2,1,0:T(8,128)(2,1)} %param.13) | copy-start | bytes 786436
  82.8 234.4 %reduce-scatter.7.cloned.1.call-start = ((), (), s32[]{:S(2)}) async-start(), calls=%async_computation.5 | async-start | bytes 589824 | tf_op jit(solution)/shard_map/reduce_scatter | solution.py:86
Sparse Core Ops, SparseCore 0:
  9.8 57.6 all-gather.1
  76.0 59.5 reduce-scatter.8
  138.1 60.3 reduce-scatter.10
  201.0 69.4 reduce-scatter.4
  273.3 43.7 reduce-scatter.6
where the time goes:
time: 324 us
  waiting for transfers between devices  231 us (71%)
  blocking collectives  40.5 us (12%)
  between operations  15.2 us (5%)
  matrix products  13.9 us (4%)
  other arithmetic  12.4 us (4%)
  local copies, waits for them, and re-layouts  10.5 us (3%)
    reduce_scatter x1, waiting for transfers between devices, shards(): lax.psum_scatter(sum_value, 'dp', scatter_dimension=0, tiled=True)  60.3 us
    all_gather x1, waiting for transfers between devices, shards(): lax.all_gather(enc_out, 'seq', axis=2, tiled=True)[0]  55.8 us
    reduce_scatter x1, waiting for transfers between devices, shards(): lax.psum_scatter(sum_key, 'dp', scatter_dimension=0, tiled=True)  52.7 us
    psum x1, blocking collectives, shards(): lax.psum((jnp.sum(share_key * share_key), jnp.sum(share_value * share_val...  40.5 us
    reduce_scatter x1, waiting for transfers between devices, shards(): lax.psum_scatter(by_section, 'seq', scatter_dimension=1, tiled=True)  33.9 us
    reduce_scatter x1, waiting for transfers between devices, shards(): lax.psum_scatter(lax.dot_general(section_wkey, keys_flat, column_contract...  26.8 us
    unnamed x14, local copies, waits for them, and re-layouts  6.71 us
  transfers between devices with their start and end apart: 5, of which 5 were waited for; matrix products, arithmetic and copies ran while one was open for 9% of the time, Pallas kernels for 0%

commit v1 on v0

--- a/solution.py
+++ b/solution.py
@@ -7,6 +7,11 @@
 D = 4096
 H = 8
 HD = 256
+
+
+def gather_over(x, name, d):
+    repeated = jnp.stack([x] * lax.axis_size(name))
+    return jnp.concatenate(lax.all_to_all(repeated, name, 0, 0), axis=d)
 
 
 def head_backward(query_heads, key_heads, value_heads, grad_heads, dec_ids, enc_ids):
@@ -88,7 +93,7 @@
     token_contract = (((0,), (0,)), ((), ()))
     grad_both = jnp.concatenate([keys_flat, values_flat], axis=1)
     both_sums = lax.dot_general(
-        lax.all_gather(enc_out, "seq", axis=2, tiled=True)[0],
+        gather_over(enc_out, "seq", 2)[0],
         grad_both,
         token_contract,
         preferred_element_type=jnp.float32,

time: 324 us -> 371 us (1.15)
  waiting for transfers between devices: 231 us -> 266 us
  starting transfers between devices: 0.2 us -> 8.77 us
    all_to_all x0 -> x1, waiting for transfers between devices: none -> 93.9 us  [gather_over(): return jnp.concatenate(lax.all_to_all(repeated, name, 0, 0), axis=d)]
    all_gather x1 -> x0, waiting for transfers between devices: 55.8 us -> none  [shards(): lax.all_gather(enc_out, 'seq', axis=2, tiled=True)[0]]
    all_to_all x0 -> x1, starting transfers between devices: none -> 8.61 us  [gather_over(): return jnp.concatenate(lax.all_to_all(repeated, name, 0, 0), axis=d)]
    another operation x0 -> x2, local copies, waits for them, and re-layouts: none -> 3.73 us  [the longest x1 2.33 us: gather_over(): repeated = jnp.stack([x] * lax.axis_size(name))]
  transfers between devices with their start and end apart: 5 -> 5, of which waited for: 5 -> 5; matrix products, arithmetic and copies ran while one was open for 9% -> 7% of each run, Pallas kernels for 0% -> 0%
where the time goes in v1:
time: 371 us; the launch traced here: 370 us
  waiting for transfers between devices  266 us (72%)
  blocking collectives  40.5 us (11%)
  between operations  15.2 us (4%)
  local copies, waits for them, and re-layouts  13.9 us (4%)
  matrix products  12.9 us (3%)
  other arithmetic  12.4 us (3%)
  starting transfers between devices  8.77 us (2%)
    all_to_all x1, waiting for transfers between devices, gather_over(): return jnp.concatenate(lax.all_to_all(repeated, name, 0, 0), axis=d)  93.9 us
    reduce_scatter x1, waiting for transfers between devices, shards(): lax.psum_scatter(sum_value, 'dp', scatter_dimension=0, tiled=True)  60.3 us
    reduce_scatter x1, waiting for transfers between devices, shards(): lax.psum_scatter(sum_key, 'dp', scatter_dimension=0, tiled=True)  50.4 us
    psum x1, blocking collectives, shards(): lax.psum((jnp.sum(share_key * share_key), jnp.sum(share_value * share_val...  40.5 us
    reduce_scatter x1, waiting for transfers between devices, shards(): lax.psum_scatter(by_section, 'seq', scatter_dimension=1, tiled=True)  33.7 us
    reduce_scatter x1, waiting for transfers between devices, shards(): lax.psum_scatter(lax.dot_general(section_wkey, keys_flat, column_contract...  27.2 us
    all_to_all x1, starting transfers between devices, gather_over(): return jnp.concatenate(lax.all_to_all(repeated, name, 0, 0), axis=d)  8.61 us
  transfers between devices with their start and end apart: 5, of which 5 were waited for; matrix products, arithmetic and copies ran while one was open for 7% of the time, Pallas kernels for 0%

profile of v1, /device:TPU:4, one launch (start us, length us, event | category | flops | bytes accessed | tf_op | source)
XLA Modules:
  0.0 370.0 jit_solution(9147246999617725597)
XLA Ops:
  7.2 0.0 copy-start
  7.2 1.4 copy.18
  8.6 2.3 stack.2
  10.9 0.0 copy-start.2
  10.9 0.0 copy-start.5
  10.9 0.0 copy-start.7
  10.9 0.0 copy-start.8
  10.9 8.6 %all-to-all-start = ((bf16[8,1,512,512]{2,3,1,0:T(8,128)(2,1)}), bf16[8,1,512,512]{2,3,1,0:T(8,128)(2,1)}, u32[]{:S(2)}, u32[]{:S(2)}) async-start(bf16[8,1,512,512]{2,3,1,0:T(8,128)(2,1)} %stack.2), calls=%async_computation.2 | async-start | bytes 8388608 | tf_op jit(solution)/shard_map/all_to_all | solution.py:14
  19.5 0.0 copy-start.3
  19.5 0.0 copy-start.4
  19.6 0.0 reduce-scatter.9.cloned.1.call-start
  19.6 0.0 copy-done.2
  19.6 0.0 copy-done.5
  19.6 0.0 copy-done.7
  19.6 0.0 copy-done.8
  19.6 0.3 fusion.22
  20.0 0.2 fusion.6
  20.2 0.3 copy-done.3
  20.5 0.1 copy-done.4
  20.6 0.4 multiply_reduce_fusion.2
  20.9 0.3 multiply_convert_fusion
  21.2 0.3 convolution_convert_fusion.1
  21.6 0.4 convolution_convert_fusion
  22.0 93.9 %all-to-all-done = bf16[8,1,512,512]{2,3,1,0:T(8,128)(2,1)} async-done(((bf16[8,1,512,512]{2,3,1,0:T(8,128)(2,1)}), bf16[8,1,512,512]{2,3,1,0:T(8,128)(2,1)}, u32[]{:S(2)}, u32[]{:S(2)}) %all-to-all-start) | async-done | bytes 4194336 | tf_op jit(solution)/shard_map/all_to_all | solution.py:14
  115.9 4.6 %convolution_bitcast_fusion = f32[4096,512]{0,1:T(8,128)S(1)} fusion(bf16[512,4096]{0,1:T(8,128)(2,1)} %bitcast.18, bf16[512,256]{0,1:T(8,128)(2,1)S(1)} %convolution_convert_fusion, bf16[512,256]{0,1:T(8,128)(2,1)S(1)} %convolution_convert_fusion.1), kind=kOutput, calls=%fused_computation.1 | convolution fusion | flops 2148532224 | bytes 13107200 | tf_op jit(solution)/shard_map/dot_general | solution.py:95
  120.5 3.8 %fusion.21 = (f32[4096,256]{0,1:T(8,128)}, f32[4096,256]{0,1:T(8,128)}) fusion(f32[4096,512]{0,1:T(8,128)S(1)} %convolution_bitcast_fusion), kind=kLoop, calls=%fused_computation.33 | loop fusion | bytes 16777216 | tf_op jit(solution)/shard_map/slice | solution.py:102
  124.2 0.0 reduce-scatter.9.cloned.1.call-update
  124.3 0.0 reduce-scatter.11.cloned.1.call-start
  124.3 0.7 reduce-scatter.11.cloned.1.call-update
  125.0 0.0 reduce-scatter.5.cloned.1.call-start
  125.1 0.0 copy-done
  125.1 0.0 copy-start.1
  125.1 1.3 fusion.1
  126.4 0.3 copy-done.1
  126.7 4.5 %add_bitcast_fusion = f32[4096,512]{0,1:T(8,128)} fusion(f32[512,4096]{1,0:T(8,128)S(1)} %fusion.1, bf16[512,256]{0,1:T(8,128)(2,1)S(1)} %convolution_convert_fusion, bf16[1,4096,256]{2,1,0:T(8,128)(2,1)S(1)} %copy-done.1), kind=kOutput, calls=%fused_computation | convolution fusion | flops 1075838976 | bytes 19136512 | tf_op jit(solution)/shard_map/dot_general | solution.py:84
  131.2 0.0 reduce-scatter.5.cloned.1.call-update
  131.2 0.0 copy-start.6
  131.2 0.0 reduce-scatter.7.cloned.1.call-start
  131.3 50.4 %reduce-scatter.9.cloned.1.call-done = f32[2048,256]{0,1:T(8,128)} async-done(((f32[4096,256]{0,1:T(8,128)}), f32[2048,256]{0,1:T(8,128)}) %reduce-scatter.9.cloned.1.call-update) | async-done | bytes 2097168 | tf_op jit(solution)/shard_map/reduce_scatter | solution.py:104
  181.7 2.7 multiply_reduce_fusion.1
  184.4 60.3 %reduce-scatter.11.cloned.1.call-done = f32[2048,256]{0,1:T(8,128)} async-done(((f32[4096,256]{0,1:T(8,128)}), f32[2048,256]{0,1:T(8,128)}) %reduce-scatter.11.cloned.1.call-update) | async-done | bytes 2097168 | tf_op jit(solution)/shard_map/reduce_scatter | solution.py:105
  244.7 2.7 multiply_reduce_fusion
  247.5 0.0 copy-done.6
  247.5 1.1 fusion.4
  248.5 40.5 %all-reduce = (f32[]{:T(128)}, f32[]{:T(128)}) all-reduce(f32[]{:T(128)} %multiply_reduce_fusion.1, f32[]{:T(128)} %multiply_reduce_fusion), channel_id=1, replica_groups=mesh['dp'=2,'pipe'=16,'seq'=8] {'dp','seq'}, use_global_device_ids=true, to_apply=%region_7.8 | all-reduce | flops 2 | bytes 16 | tf_op jit(solution)/shard_map/psum | solution.py:107
  289.7 27.2 %reduce-scatter.5.cloned.1.call-done = f32[256,512]{0,1:T(8,128)} async-done(((f32[4096,512]{0,1:T(8,128)}), f32[256,512]{0,1:T(8,128)}) %reduce-scatter.5.cloned.1.call-update) | async-done | bytes 524304 | tf_op jit(solution)/shard_map/reduce_scatter | solution.py:80
  316.9 0.0 reduce-scatter.7.cloned.1.call-update
  316.9 3.2 divide_bitcast_fusion.1
  320.1 2.9 copy.20
  323.6 3.2 divide_bitcast_fusion
  326.8 2.9 copy.21
  329.7 33.7 %reduce-scatter.7.cloned.1.call-done = f32[256,64]{0,1:T(8,128)} async-done(((f32[256,512]{0,1:T(8,128)}), f32[256,64]{0,1:T(8,128)}) %reduce-scatter.7.cloned.1.call-update) | async-done | bytes 65552 | tf_op jit(solution)/shard_map/reduce_scatter | solution.py:91
Async XLA Ops:
  7.2 117.9 %copy-start = (bf16[1,4096,256]{2,1,0:T(8,128)(2,1)S(1)}, bf16[1,4096,256]{2,1,0:T(8,128)(2,1)}, u32[]{:S(2)}) copy-start(bf16[1,4096,256]{2,1,0:T(8,128)(2,1)} %param.10) | copy-start | bytes 6291460
  10.9 8.7 %copy-start.2 = (bf16[1,1,512,256]{3,2,1,0:T(8,128)(2,1)S(1)}, bf16[1,1,512,256]{3,2,1,0:T(8,128)(2,1)}, u32[]{:S(2)}) copy-start(bf16[1,1,512,256]{3,2,1,0:T(8,128)(2,1)} %param.12) | copy-start | bytes 786436
  10.9 8.7 %copy-start.5 = (bf16[1,1,512,256]{3,2,1,0:T(8,128)(2,1)S(1)}, bf16[1,1,512,256]{3,2,1,0:T(8,128)(2,1)}, u32[]{:S(2)}) copy-start(bf16[1,1,512,256]{3,2,1,0:T(8,128)(2,1)} %param.13) | copy-start | bytes 786436
  10.9 8.7 %copy-start.7 = (s32[1,512]{1,0:T(1,128)S(1)}, s32[1,512]{1,0:T(1,128)}, u32[]{:S(2)}) copy-start(s32[1,512]{1,0:T(1,128)} %param.17) | copy-start | bytes 6148
  10.9 8.7 %copy-start.8 = (s32[1,512]{1,0:T(1,128)S(1)}, s32[1,512]{1,0:T(1,128)}, u32[]{:S(2)}) copy-start(s32[1,512]{1,0:T(1,128)} %param.16) | copy-start | bytes 6148
  10.9 105.0 %all-to-all-start = ((bf16[8,1,512,512]{2,3,1,0:T(8,128)(2,1)}), bf16[8,1,512,512]{2,3,1,0:T(8,128)(2,1)}, u32[]{:S(2)}, u32[]{:S(2)}) async-start(bf16[8,1,512,512]{2,3,1,0:T(8,128)(2,1)} %stack.2), calls=%async_computation.2 | async-start | bytes 8388608 | tf_op jit(solution)/shard_map/all_to_all | solution.py:14
  19.5 0.9 copy-start.3
  19.5 1.0 copy-start.4
  19.6 162.2 %reduce-scatter.9.cloned.1.call-start = ((), (), s32[]{:S(2)}) async-start(), calls=%async_computation.7 | async-start | bytes 6291456 | tf_op jit(solution)/shard_map/reduce_scatter | solution.py:104
  124.3 120.5 %reduce-scatter.11.cloned.1.call-start = ((), (), s32[]{:S(2)}) async-start(), calls=%async_computation.8 | async-start | bytes 6291456 | tf_op jit(solution)/shard_map/reduce_scatter | solution.py:105
  125.0 191.9 %reduce-scatter.5.cloned.1.call-start = ((), (), s32[]{:S(2)}) async-start(), calls=%async_computation.5 | async-start | bytes 8912896 | tf_op jit(solution)/shard_map/reduce_scatter | solution.py:80
  125.1 1.6 copy-start.1
  131.2 116.2 %copy-start.6 = (bf16[1,1,512,256]{3,2,1,0:T(8,128)(2,1)S(1)}, bf16[1,1,512,256]{3,2,1,0:T(8,128)(2,1)}, u32[]{:S(2)}) copy-start(bf16[1,1,512,256]{3,2,1,0:T(8,128)(2,1)} %param.13) | copy-start | bytes 786436
  131.2 232.2 %reduce-scatter.7.cloned.1.call-start = ((), (), s32[]{:S(2)}) async-start(), calls=%async_computation.6 | async-start | bytes 589824 | tf_op jit(solution)/shard_map/reduce_scatter | solution.py:91
Sparse Core Ops, SparseCore 0:
  124.4 57.2 reduce-scatter.8
  184.3 60.4 reduce-scatter.10
  247.3 69.5 reduce-scatter.4
  319.8 43.5 reduce-scatter.6
